TPU v7x, 32 devices: a whole 2x2x4 slice. The times are simulated.
32 devices in a mesh: wide: 8 (over y, x, core), narrow: 4 (over z).
Axes of the slice: x: 2, y: 2, z: 4, core: 2. Of those that a mesh axis runs over, the one named last changes fastest.
Arguments:
- hidden_in: bfloat16 [4096, 1536], P('wide'), may hold values from -64 to 64
- segment_ids: int32 [4096], P('wide'), may hold values from 0 to 7, as said below
- seg_lengths: int32 [8], replicated, may hold values from 1 to 2048, as said below
- seg_offsets: int32 [8], replicated, may hold values from 0 to 4095, as said below
- block_table: int32 [8, 16], replicated, may hold values from -1 to 39, as said below
- attn_gain: bfloat16 [1536], replicated, may hold values from 0.099609375 to 1.8984375
- w_query: bfloat16 [1536, 1536], P('wide', 'narrow'), may hold values from -0.15625 to 0.15625
- b_query: bfloat16 [1536], P('narrow'), may hold values from -128 to 128
- w_keyval: bfloat16 [1536, 512], P('wide'), may hold values from -0.15625 to 0.15625
- b_keyval: bfloat16 [512], replicated, may hold values from -128 to 128
- w_out: bfloat16 [1536, 1536], P('narrow', 'wide'), may hold values from -0.15625 to 0.15625
- mlp_gain: bfloat16 [1536], replicated, may hold values from 0.099609375 to 1.8984375
- w_gate: bfloat16 [1536, 8960], P('wide', 'narrow'), may hold values from -0.15625 to 0.15625
- w_up: bfloat16 [1536, 8960], P('wide', 'narrow'), may hold values from -0.15625 to 0.15625
- w_down: bfloat16 [8960, 1536], P('narrow', 'wide'), may hold values from -0.0625 to 0.0625
- next_gain: bfloat16 [1536], replicated, may hold values from 0.099609375 to 1.8984375
- w_query2: bfloat16 [1536, 1536], P('wide', 'narrow'), may hold values from -0.15625 to 0.15625
- b_query2: bfloat16 [1536], P('narrow'), may hold values from -3 to 3
- w_keyval2: bfloat16 [1536, 512], P('wide'), may hold values from -0.15625 to 0.15625
- b_keyval2: bfloat16 [512], replicated, may hold values from -3 to 3
Outputs:
- hidden_out: bfloat16 [4096, 1536], P('wide')
- next_query: bfloat16 [4096, 1536], P('wide', 'narrow')
- next_keyval: bfloat16 [4096, 512], P('wide', 'narrow')
- kv_cache: bfloat16 [4, 40, 128, 128], P('narrow', 'wide')
Inputs may be any that keep to these rules, and one draw needn't show every extreme that they name: `segment_ids`: segment s covers tokens seg_offsets[s] to seg_offsets[s] + seg_lengths[s] - 1. `seg_lengths`: they sum to 4096. seg_offsets[0] = 0 and seg_offsets[s + 1] = seg_offsets[s] + seg_lengths[s]. `block_table`: entry j of row s is a page for j below ceil(seg_lengths[s] / 128) and -1 beyond; no page appears twice.
All inputs are finite; a program needn't handle non-finite values.
Results may differ from a plain program's by a relative error of at most 0.017.
Values may be sent and summed in bfloat16 or wider, within the bound.
No kernel may reach another device: no remote copies, remote signals or barrier semaphores. Data moves between devices by JAX's collectives and lax.ppermute only.
A program may use at most 128 MiB of HBM per device.

v0:
```python
import math
import jax
import jax.numpy as jnp
from jax import lax
from jax.sharding import PartitionSpec as P

HD = 128
PAGE_LEN = 128
norm_eps = 1e-06
rope_base = 1000000.0
masked_score = -1e30


def rms_norm(activations, gain_vector):
    values = activations.astype(jnp.float32)
    row_scale = lax.rsqrt(jnp.mean(values * values, axis=-1, keepdims=True) + norm_eps)
    return (values * row_scale * gain_vector.astype(jnp.float32)).astype(jnp.bfloat16)


def rotate(values, positions):
    half_dim = values.shape[-1] // 2
    frequency = rope_base ** (-(jnp.arange(half_dim, dtype=jnp.float32) * 2.0 / values.shape[-1]))
    angles = positions.astype(jnp.float32)[:, None, None] * frequency
    cosine = jnp.cos(angles)
    sine_part = jnp.sin(angles)
    lower_half = values[..., :half_dim]
    upper_half = values[..., half_dim:]
    return jnp.concatenate(
        [
            lower_half * cosine - upper_half * sine_part,
            upper_half * cosine + lower_half * sine_part,
        ],
        axis=-1,
    )


def lookup(table, indices):
    table_match = indices[..., None] == jnp.arange(table.shape[0], dtype=jnp.int32)
    return jnp.sum(jnp.where(table_match, table, 0), axis=-1)


def fold_rows(normed, first_weight, second_weight):
    return (
        jnp.dot(
            normed,
            lax.all_gather(first_weight, "wide", axis=0, tiled=True),
            preferred_element_type=jnp.float32,
        ),
        jnp.dot(
            normed,
            lax.all_gather(second_weight, "wide", axis=0, tiled=True),
            preferred_element_type=jnp.float32,
        ),
    )


def column_terms(left_rows, weight_block):
    return jnp.dot(
        left_rows,
        lax.all_gather(weight_block, "wide", axis=1, tiled=True),
        preferred_element_type=jnp.float32,
    )


def keyval_block(w_keyval, b_keyval, head_pair):
    pair_width = 2 * HD
    pair_offset = head_pair * pair_width
    return (w_keyval, b_keyval, pair_offset)


def add_branch(partial_terms, base_rows, narrow_index):
    share_sum = lax.psum_scatter(
        partial_terms.astype(jnp.bfloat16), "narrow", scatter_dimension=1, tiled=True
    ).astype(jnp.float32)
    share_width = share_sum.shape[1]
    base_share = lax.dynamic_slice_in_dim(base_rows, narrow_index * share_width, share_width, 1)
    updated = (base_share.astype(jnp.float32) + share_sum).astype(jnp.bfloat16)
    result_rows = lax.all_gather(updated, "narrow", axis=1, tiled=True)
    return result_rows


def attend(queries, keys_all, values_all, segment_ids, seg_offsets, row_base):
    tok_rows = queries.shape[0]
    local_heads = queries.shape[1] // HD
    total_rows = keys_all.shape[0]
    key_block = math.gcd(total_rows, 512)
    score_scale = HD ** (-0.5)
    stacked = (
        queries.reshape(tok_rows, local_heads, HD)
        .transpose(1, 0, 2)
        .reshape(local_heads * tok_rows, HD)
    )
    query_pos = row_base + jnp.arange(tok_rows, dtype=jnp.int32)
    query_pos_all = jnp.tile(query_pos, local_heads)
    query_seg_all = jnp.tile(segment_ids, local_heads)
    lowest = lookup(seg_offsets, segment_ids[:1])[0]
    first_block = lowest // key_block
    last_block = (row_base + tok_rows - 1) // key_block

    def visit_block(block_number, state_now):
        running_max, running_sum, accumulated = state_now
        key_start = block_number * key_block
        keys_here = lax.dynamic_slice_in_dim(keys_all, key_start, key_block, 0)
        values_here = lax.dynamic_slice_in_dim(values_all, key_start, key_block, 0)
        key_pos = key_start + jnp.arange(key_block, dtype=jnp.int32)
        key_seg = jnp.sum((key_pos[:, None] >= seg_offsets[None, 1:]).astype(jnp.int32), axis=1)
        visible = (
            (key_seg[None, :] == query_seg_all[:, None])
            & (key_pos[None, :] <= query_pos_all[:, None])
            & (key_pos[None, :] >= 0)
        )
        scores = (
            jnp.einsum("qd,kd->qk", stacked, keys_here, preferred_element_type=jnp.float32)
            * score_scale
        )
        scores = jnp.where(visible, scores, masked_score)
        new_max = jnp.maximum(running_max, jnp.max(scores, axis=1))
        weights = jnp.where(visible, jnp.exp(scores - new_max[:, None]), 0.0)
        factor = jnp.exp(running_max - new_max)
        running_sum = running_sum * factor + jnp.sum(weights, axis=1)
        accumulated = accumulated * factor[:, None] + jnp.dot(
            weights.astype(jnp.bfloat16), values_here, preferred_element_type=jnp.float32
        )
        return (new_max, running_sum, accumulated)

    row_count = stacked.shape[0]
    initial = (
        jnp.full((row_count,), masked_score, jnp.float32),
        jnp.zeros((row_count,), jnp.float32),
        jnp.zeros((row_count, HD), jnp.float32),
    )
    final_max, final_sum, accumulated = lax.fori_loop(
        first_block, last_block + 1, visit_block, initial
    )
    mixed_heads = (
        (accumulated / final_sum[:, None]).reshape(local_heads, tok_rows, HD).transpose(1, 0, 2)
    )
    return mixed_heads.reshape(tok_rows, local_heads * HD).astype(jnp.bfloat16)


def fill_pages(source, seg_lengths, seg_offsets, block_table, first_page, page_count):
    pages_here = first_page + jnp.arange(page_count, dtype=jnp.int32)
    page_match = block_table[None, :, :] == pages_here[:, None, None]
    seg_grid = jnp.arange(block_table.shape[0], dtype=jnp.int32)[None, :, None]
    page_grid = jnp.arange(block_table.shape[1], dtype=jnp.int32)[None, None, :]
    page_owner = jnp.sum(jnp.where(page_match, seg_grid, 0), axis=(1, 2))
    logical = jnp.sum(jnp.where(page_match, page_grid, 0), axis=(1, 2))
    in_use = jnp.any(page_match, axis=(1, 2))
    first_token = lookup(seg_offsets, page_owner) + logical * PAGE_LEN
    filled = lookup(seg_lengths, page_owner) - logical * PAGE_LEN
    slot_index = jnp.arange(PAGE_LEN, dtype=jnp.int32)
    row_ids = jnp.clip(first_token[:, None] + slot_index[None, :], 0, source.shape[0] - 1)
    keep_slot = in_use[:, None] & (slot_index[None, :] < filled[:, None])
    taken_rows = jnp.take(source, row_ids.reshape(-1), axis=0).reshape(
        page_count, PAGE_LEN, source.shape[1]
    )
    return jnp.where(keep_slot[:, :, None], taken_rows, jnp.zeros((), source.dtype))


def local(
    hidden_in,
    segment_ids,
    seg_lengths,
    seg_offsets,
    block_table,
    attn_gain,
    w_query,
    b_query,
    w_keyval,
    b_keyval,
    w_out,
    mlp_gain,
    w_gate,
    w_up,
    w_down,
    next_gain,
    w_query2,
    b_query2,
    w_keyval2,
    b_keyval2,
):
    tok_rows = hidden_in.shape[0]
    wide_index = lax.axis_index("wide")
    narrow_index = lax.axis_index("narrow")
    head_pair = narrow_index // 2
    kind_index = narrow_index % 2
    row_base = wide_index * tok_rows
    positions = row_base + jnp.arange(tok_rows, dtype=jnp.int32) - lookup(seg_offsets, segment_ids)
    normed = rms_norm(hidden_in, attn_gain)
    kv_weight, kv_bias, pair_offset = keyval_block(w_keyval, b_keyval, head_pair)
    query_sum, keyval_sum = fold_rows(normed, w_query, kv_weight)
    queries = query_sum + b_query.astype(jnp.float32)
    local_heads = queries.shape[1] // HD
    queries = (
        rotate(queries.reshape(tok_rows, local_heads, HD), positions)
        .reshape(tok_rows, local_heads * HD)
        .astype(jnp.bfloat16)
    )
    keyvals = (keyval_sum + kv_bias.astype(jnp.float32)).reshape(tok_rows, -1, 2, HD)
    keyvals = jnp.stack([rotate(keyvals[:, :, 0, :], positions), keyvals[:, :, 1, :]], axis=2)
    keyvals = keyvals.reshape(tok_rows, kv_weight.shape[1]).astype(jnp.bfloat16)
    gathered = lax.all_gather(keyvals, "wide", axis=0, tiled=True)
    source = lax.dynamic_slice_in_dim(gathered, pair_offset + kind_index * HD, HD, 1)
    keys_all = lax.dynamic_slice_in_dim(gathered, pair_offset, HD, 1)
    values_all = lax.dynamic_slice_in_dim(gathered, pair_offset + HD, HD, 1)
    mixed_heads = attend(queries, keys_all, values_all, segment_ids, seg_offsets, row_base)
    residual = add_branch(column_terms(mixed_heads, w_out), hidden_in, narrow_index)
    normed_mlp = rms_norm(residual, mlp_gain)
    gate_sum, up_sum = fold_rows(normed_mlp, w_gate, w_up)
    hidden_units = (jax.nn.silu(gate_sum) * up_sum).astype(jnp.bfloat16)
    hidden_out = add_branch(column_terms(hidden_units, w_down), residual, narrow_index)
    normed_next = rms_norm(hidden_out, next_gain)
    kv_weight_next, kv_bias_next, pair_offset_next = keyval_block(w_keyval2, b_keyval2, head_pair)
    query_next, keyval_next = fold_rows(normed_next, w_query2, kv_weight_next)
    next_query = (query_next + b_query2.astype(jnp.float32)).astype(jnp.bfloat16)
    keyval_next = keyval_next + kv_bias_next.astype(jnp.float32)
    next_keyval = lax.dynamic_slice_in_dim(
        keyval_next, pair_offset_next + kind_index * HD, HD, 1
    ).astype(jnp.bfloat16)
    page_count = tok_rows // PAGE_LEN + 1
    cache_block = fill_pages(
        source, seg_lengths, seg_offsets, block_table, wide_index * page_count, page_count
    )
    return (hidden_out, next_query, next_keyval, cache_block[None])


def solution(mesh):
    placed = (
        P("wide", None),
        P("wide"),
        P(),
        P(),
        P(),
        P(),
        P("wide", "narrow"),
        P("narrow"),
        P("wide", None),
        P(),
        P("narrow", "wide"),
        P(),
        P("wide", "narrow"),
        P("wide", "narrow"),
        P("narrow", "wide"),
        P(),
        P("wide", "narrow"),
        P("narrow"),
        P("wide", None),
        P(),
    )
    return jax.shard_map(
        local,
        mesh=mesh,
        in_specs=placed,
        out_specs=(
            P("wide", None),
            P("wide", "narrow"),
            P("wide", "narrow"),
            P("narrow", "wide", None, None),
        ),
        check_vma=False,
    )
```

profile of v0, /device:TPU:0, one launch (start us, length us, event | category | flops | bytes accessed | tf_op | source)
XLA Modules:
  0.0 521.2 jit_solution(14658357420002267087)
XLA Ops:
  13.2 25.1 %all-gather.12.cloned.1.call-done = bf16[1536,512]{1,0:T(8,128)(2,1)} async-done(((bf16[192,512]{1,0:T(8,128)(2,1)}), bf16[1536,512]{1,0:T(8,128)(2,1)}) %all-gather.12.cloned.1.call-update) | async-done | bytes 1572880 | tf_op jit(solution)/shard_map/all_gather | solution.py:51
  38.3 3.0 convolution_add_fusion.1
  47.8 16.5 %all-gather.16.cloned.1.call-done = bf16[1536,384]{1,0:T(8,128)(2,1)} async-done(((bf16[192,384]{1,0:T(8,128)(2,1)}), bf16[1536,384]{1,0:T(8,128)(2,1)}) %all-gather.16.cloned.1.call-update) | async-done | bytes 1179664 | tf_op jit(solution)/shard_map/all_gather | solution.py:46
  64.3 2.2 convolution_add_fusion.3
  66.9 36.6 %all-gather.14.cloned.1.call-done = bf16[4096,512]{1,0:T(8,128)(2,1)} async-done(((bf16[512,512]{1,0:T(8,128)(2,1)}), bf16[4096,512]{1,0:T(8,128)(2,1)}) %all-gather.14.cloned.1.call-update) | async-done | bytes 4194320 | tf_op jit(solution)/shard_map/all_gather | solution.py:202
  103.5 3.1 constant_dynamic-slice_fusion
  106.6 5.7 %while.15 = (s32[]{:T(128)}, f32[1536]{0:T(1024)S(1)}, f32[1536]{0:T(1024)S(1)}, f32[1536,128]{1,0:T(8,128)S(1)}, s32[]{:T(128)}, /*index=5*/s32[8]{0:T(128)S(1)...) while((s32[]{:T(128)}, f32[1536]{0:T(1024)S(1)}, ...), condition=%wide.region_7.8_spmd.clone, body=%wide.region_3.7_spmd.clone.sunk | while | flops 419576320 | bytes 11870495 | solution.py:132
  106.9 2.2 fusion.73
  112.8 16.5 %all-gather.18.cloned.1.call-done = bf16[384,1536]{0,1:T(8,128)(2,1)} async-done(((bf16[384,192]{0,1:T(8,128)(2,1)}), bf16[384,1536]{0,1:T(8,128)(2,1)}) %all-gather.18.cloned.1.call-update) | async-done | bytes 1179664 | tf_op jit(solution)/shard_map/all_gather | solution.py:60
  129.3 2.3 convolution_convert_fusion.1
  133.3 41.8 %reduce-scatter.7.cloned.1.call-done = bf16[384,512]{1,0:T(8,128)(2,1)} async-done(((bf16[1536,512]{1,0:T(8,128)(2,1)}), bf16[384,512]{1,0:T(8,128)(2,1)}) %reduce-scatter.7.cloned.1.call-update) | async-done | bytes 393232
  180.7 33.7 %all-gather.20.cloned.1.call-done = bf16[512,1536]{1,0:T(8,128)(2,1)} async-done(((bf16[512,384]{1,0:T(8,128)(2,1)}), bf16[512,1536]{1,0:T(8,128)(2,1)}) %all-gather.20.cloned.1.call-update) | async-done | bytes 1572880 | tf_op jit(solution)/shard_map/all_gather | solution.py:78
  216.2 47.9 %all-gather.22.cloned.1.call-done = bf16[1536,2240]{1,0:T(8,128)(2,1)} async-done(((bf16[192,2240]{1,0:T(8,128)(2,1)}), bf16[1536,2240]{1,0:T(8,128)(2,1)}) %all-gather.22.cloned.1.call-update) | async-done | bytes 6881296 | tf_op jit(solution)/shard_map/all_gather | solution.py:46
  264.2 9.5 %fusion.28 = f32[512,2240]{0,1:T(8,128)} fusion(bf16[1536,2240]{1,0:T(8,128)(2,1)} %all-gather.22.cloned.1.call-done, bf16[512,1536]{1,0:T(8,128)(2,1)} %all-gather.20.cloned.1.call-done, f32[1536]{0:T(1024)S(1)} %convert_element_type.121, f32[512]{0:T(512)S(1)} %add_rsqrt_fusion.1), kind=kOutput, calls=%fused_computation.52 | convolution fusion | flops 3526361088 | bytes 13049856 | tf_op jit(solution)/shard_map/dot_general | solution.py:44
  273.6 41.3 %all-gather.24.cloned.1.call-done = bf16[1536,2240]{1,0:T(8,128)(2,1)} async-done(((bf16[192,2240]{1,0:T(8,128)(2,1)}), bf16[1536,2240]{1,0:T(8,128)(2,1)}) %all-gather.24.cloned.1.call-update) | async-done | bytes 6881296 | tf_op jit(solution)/shard_map/all_gather | solution.py:51
  314.9 50.8 %all-gather.26.cloned.1.call-done = bf16[2240,1536]{0,1:T(8,128)(2,1)} async-done(((bf16[2240,192]{0,1:T(8,128)(2,1)}), bf16[2240,1536]{0,1:T(8,128)(2,1)}) %all-gather.26.cloned.1.call-update) | async-done | bytes 6881296 | tf_op jit(solution)/shard_map/all_gather | solution.py:60
  365.7 15.9 %convolution_convert_fusion = bf16[512,1536]{1,0:T(8,128)(2,1)} fusion(bf16[2240,1536]{0,1:T(8,128)(2,1)} %all-gather.26.cloned.1.call-done, bf16[1536,2240]{1,0:T(8,128)(2,1)} %all-gather.24.cloned.1.call-done, f32[512,2240]{0,1:T(8,128)} %fusion.28, bf16[512,1536]{1,0:T(8,128)(2,1)S(1)} %copy-done.2, f32[1536]{0:T(1024)S(1)} %convert_element_type.121, ...), kind=kOutput, calls=%fused_computation.40 | convolution fusion | flops 7057244160 | bytes 21504000 | tf_op jit(solution)/shard_map/dot_general | solution.py:58
  381.6 2.7 copy.45
  384.4 35.4 %reduce-scatter.9.cloned.1.call-done = bf16[384,512]{1,0:T(8,128)(2,1)} async-done(((bf16[1536,512]{1,0:T(8,128)(2,1)}), bf16[384,512]{1,0:T(8,128)(2,1)}) %reduce-scatter.9.cloned.1.call-update) | async-done | bytes 393232
  427.2 30.9 %all-gather.28.cloned.1.call-done = bf16[512,1536]{1,0:T(8,128)(2,1)} async-done(((bf16[512,384]{1,0:T(8,128)(2,1)}), bf16[512,1536]{1,0:T(8,128)(2,1)}) %all-gather.28.cloned.1.call-update) | async-done | bytes 1572880 | tf_op jit(solution)/shard_map/all_gather | solution.py:78
  459.9 24.6 %all-gather.32.cloned.1.call-done = bf16[1536,512]{1,0:T(8,128)(2,1)} async-done(((bf16[192,512]{1,0:T(8,128)(2,1)}), bf16[1536,512]{1,0:T(8,128)(2,1)}) %all-gather.32.cloned.1.call-update) | async-done | bytes 1572880 | tf_op jit(solution)/shard_map/all_gather | solution.py:51
  484.5 2.9 fusion.30
  488.1 22.4 %all-gather.30.cloned.1.call-done = bf16[1536,384]{1,0:T(8,128)(2,1)} async-done(((bf16[192,384]{1,0:T(8,128)(2,1)}), bf16[1536,384]{1,0:T(8,128)(2,1)}) %all-gather.30.cloned.1.call-update) | async-done | bytes 1179664 | tf_op jit(solution)/shard_map/all_gather | solution.py:46
  510.5 3.0 fusion.26
  (115 shorter events, 34.0 us)
Async XLA Ops:
  7.2 31.1 %all-gather.12.cloned.1.call-start = ((), (), s32[]{:S(2)}) async-start(), calls=%async_computation.2 | async-start | bytes 1769472 | tf_op jit(solution)/shard_map/all_gather | solution.py:51
  7.9 56.4 %all-gather.16.cloned.1.call-start = ((), (), s32[]{:S(2)}) async-start(), calls=%async_computation.4 | async-start | bytes 1327104 | tf_op jit(solution)/shard_map/all_gather | solution.py:46
  8.6 94.9 %all-gather.14.cloned.1.call-start = ((), (), s32[]{:S(2)}) async-start(), calls=%async_computation.3 | async-start | bytes 4718592 | tf_op jit(solution)/shard_map/all_gather | solution.py:202
  41.3 2.5 copy-start.7
  41.3 6.4 %copy-start.8 = (bf16[384]{0:T(512)(128)(2,1)S(1)}, bf16[384]{0:T(512)(128)(2,1)}, u32[]{:S(2)}) copy-start(bf16[384]{0:T(512)(128)(2,1)} %param.29) | copy-start | bytes 2308
  41.3 22.9 %copy-start.1 = (bf16[512,1536]{1,0:T(8,128)(2,1)S(1)}, bf16[512,1536]{1,0:T(8,128)(2,1)}, u32[]{:S(2)}) copy-start(bf16[512,1536]{1,0:T(8,128)(2,1)} %param.22) | copy-start | bytes 4718596
  42.7 86.7 %all-gather.18.cloned.1.call-start = ((), (), s32[]{:S(2)}) async-start(), calls=%async_computation.5 | async-start | bytes 1327104 | tf_op jit(solution)/shard_map/all_gather | solution.py:60
  43.2 131.9 %reduce-scatter.7.cloned.1.call-start = ((), (), s32[]{:S(2)}) async-start(), calls=%async_computation.13 | async-start | bytes 1966080
  133.2 47.5 %copy-start.5 = (bf16[1536]{0:T(1024)(128)(2,1)S(1)}, bf16[1536]{0:T(1024)(128)(2,1)}, u32[]{:S(2)}) copy-start(bf16[1536]{0:T(1024)(128)(2,1)} %param.33) | copy-start | bytes 9220
  133.3 81.2 %all-gather.20.cloned.1.call-start = ((), (), s32[]{:S(2)}) async-start(), calls=%async_computation.6 | async-start | bytes 1966080 | tf_op jit(solution)/shard_map/all_gather | solution.py:78
  178.2 85.9 %all-gather.22.cloned.1.call-start = ((), (), s32[]{:S(2)}) async-start(), calls=%async_computation.7 | async-start | bytes 7962624 | tf_op jit(solution)/shard_map/all_gather | solution.py:46
  179.0 136.0 %all-gather.24.cloned.1.call-start = ((), (), s32[]{:S(2)}) async-start(), calls=%async_computation.8 | async-start | bytes 7962624 | tf_op jit(solution)/shard_map/all_gather | solution.py:51
  179.7 186.0 %all-gather.26.cloned.1.call-start = ((), (), s32[]{:S(2)}) async-start(), calls=%async_computation.9 | async-start | bytes 7962624 | tf_op jit(solution)/shard_map/all_gather | solution.py:60
  180.5 239.3 %reduce-scatter.9.cloned.1.call-start = ((), (), s32[]{:S(2)}) async-start(), calls=%async_computation.14 | async-start | bytes 1966080
  216.2 149.5 %copy-start.2 = (bf16[512,1536]{1,0:T(8,128)(2,1)S(1)}, bf16[512,1536]{1,0:T(8,128)(2,1)}, u32[]{:S(2)}) copy-start(bf16[512,1536]{1,0:T(8,128)(2,1)} %all-gather.20.cloned.1.call-done) | copy-start | bytes 4718596
  381.6 41.6 %copy-start.4 = (s32[8,16]{1,0:T(8,128)S(1)}, s32[8,16]{1,0:T(8,128)}, u32[]{:S(2)}) copy-start(s32[8,16]{1,0:T(8,128)} %param.26) | copy-start | bytes 1540
  381.6 42.0 %copy-start.10 = (s32[8]{0:T(128)S(1)}, s32[8]{0:T(128)}, u32[]{:S(2)}) copy-start(s32[8]{0:T(128)} %param.24) | copy-start | bytes 100
  381.6 42.2 %copy-start.6 = (bf16[1536]{0:T(1024)(128)(2,1)S(1)}, bf16[1536]{0:T(1024)(128)(2,1)}, u32[]{:S(2)}) copy-start(bf16[1536]{0:T(1024)(128)(2,1)} %param.37) | copy-start | bytes 9220
  381.6 42.2 %copy-start.11 = (bf16[512]{0:T(512)(128)(2,1)S(1)}, bf16[512]{0:T(512)(128)(2,1)}, u32[]{:S(2)}) copy-start(bf16[512]{0:T(512)(128)(2,1)} %param.41) | copy-start | bytes 3076
  381.6 42.3 %copy-start.9 = (bf16[384]{0:T(512)(128)(2,1)S(1)}, bf16[384]{0:T(512)(128)(2,1)}, u32[]{:S(2)}) copy-start(bf16[384]{0:T(512)(128)(2,1)} %param.39) | copy-start | bytes 2308
  384.3 73.8 %all-gather.28.cloned.1.call-start = ((), (), s32[]{:S(2)}) async-start(), calls=%async_computation.10 | async-start | bytes 1966080 | tf_op jit(solution)/shard_map/all_gather | solution.py:78
  421.9 62.7 %all-gather.32.cloned.1.call-start = ((), (), s32[]{:S(2)}) async-start(), calls=%async_computation.12 | async-start | bytes 1769472 | tf_op jit(solution)/shard_map/all_gather | solution.py:51
  422.4 88.1 %all-gather.30.cloned.1.call-start = ((), (), s32[]{:S(2)}) async-start(), calls=%async_computation.11 | async-start | bytes 1327104 | tf_op jit(solution)/shard_map/all_gather | solution.py:46
  459.9 50.6 %copy-start = (bf16[512,1536]{1,0:T(8,128)(2,1)S(1)}, bf16[512,1536]{1,0:T(8,128)(2,1)}, u32[]{:S(2)}) copy-start(bf16[512,1536]{1,0:T(8,128)(2,1)} %all-gather.28.cloned.1.call-done) | copy-start | bytes 4718596
  (1 other events, 2.0 us)
Sparse Core Ops, SparseCore 0:
  9.9 28.3 all-gather.11
  40.2 24.0 all-gather.15
  66.8 36.7 all-gather.13
  105.2 24.0 all-gather.17
  133.4 41.7 reduce-scatter.6
  178.3 36.0 all-gather.19
  216.3 47.7 all-gather.21
  266.0 48.8 all-gather.23
  316.8 48.8 all-gather.25
  384.5 35.2 reduce-scatter.8
  422.0 36.0 all-gather.27
  459.8 24.6 all-gather.31
  486.4 24.0 all-gather.29
where the time goes:
time: 522 us; the launch traced here: 521 us
  waiting for transfers between devices  429 us (82%)
  matrix products  42.8 us (8%)
  between operations  16.9 us (3%)
  other arithmetic  16.8 us (3%)
  local copies, waits for them, and re-layouts  15.1 us (3%)
    all_gather x3, waiting for transfers between devices, fold_rows(): lax.all_gather(second_weight, 'wide', axis=0, tiled=True)  91 us
    all_gather x3, waiting for transfers between devices, fold_rows(): lax.all_gather(first_weight, 'wide', axis=0, tiled=True)  86.8 us
    unnamed x15, waiting for transfers between devices  82.5 us
    all_gather x2, waiting for transfers between devices, column_terms(): lax.all_gather(weight_block, 'wide', axis=1, tiled=True)  67.3 us
    all_gather x2, waiting for transfers between devices, add_branch(): result_rows = lax.all_gather(updated, 'narrow', axis=1, tiled=True)  64.6 us
    all_gather x1, waiting for transfers between devices, local(): gathered = lax.all_gather(keyvals, 'wide', axis=0, tiled=True)  36.6 us
    dot_general x2, matrix products, column_terms(): jnp.dot(left_rows, lax.all_gather(weight_block, 'wide', axis=1, tiled=Tru...  18.2 us
    dot_general x3, matrix products, fold_rows(): jnp.dot(normed, lax.all_gather(first_weight, 'wide', axis=0, tiled=True),...  14.7 us
  transfers between devices with their start and end apart: 13, of which 13 were waited for; matrix products, arithmetic and copies ran while one was open for 8% of the time, Pallas kernels for 0%

commit v1 on v0

--- a/solution.py
+++ b/solution.py
@@ -9,6 +9,23 @@
 norm_eps = 1e-06
 rope_base = 1000000.0
 masked_score = -1e30
+
+
+def joined_along(blocks, dim):
+    lengths = list(blocks.shape[1:])
+    lengths[dim] *= blocks.shape[0]
+    return jnp.moveaxis(blocks, 0, dim).reshape(lengths)
+
+
+def ring_gather(x, axis, dim):
+    size = lax.axis_size(axis)
+    right = [(i, (i + 1) % size) for i in range(size)]
+    blocks = [x]
+    while len(blocks) < size:
+        blocks.append(lax.ppermute(blocks[-1], axis, right))
+    index = lax.axis_index(axis)
+    blocks = jnp.stack(blocks)[(index - jnp.arange(size)) % size]
+    return joined_along(blocks, dim)
 
 
 def rms_norm(activations, gain_vector):
@@ -56,9 +73,7 @@
 
 def column_terms(left_rows, weight_block):
     return jnp.dot(
-        left_rows,
-        lax.all_gather(weight_block, "wide", axis=1, tiled=True),
-        preferred_element_type=jnp.float32,
+        left_rows, ring_gather(weight_block, "wide", 1), preferred_element_type=jnp.float32
     )
 
 

time: 522 us -> 490 us (0.939)
  waiting for transfers between devices: 429 us -> 380 us
  local copies, waits for them, and re-layouts: 15.1 us -> 31.9 us
    ppermute x0 -> x14, waiting for transfers between devices: none -> 157 us  [ring_gather(): blocks.append(lax.ppermute(blocks[-1], axis, right))]
    all_gather x2 -> x0, waiting for transfers between devices: 67.3 us -> none  [column_terms(): lax.all_gather(weight_block, 'wide', axis=1, tiled=True)]
    all_gather x3, waiting for transfers between devices: 86.8 us -> 22.4 us  [fold_rows(): lax.all_gather(first_weight, 'wide', axis=0, tiled=True)]
    all_gather x3, waiting for transfers between devices: 91 us -> 53.8 us  [fold_rows(): lax.all_gather(second_weight, 'wide', axis=0, tiled=True)]
    all_gather x2, waiting for transfers between devices: 64.6 us -> 30.9 us  [add_branch(): result_rows = lax.all_gather(updated, 'narrow', axis=1, tiled=True)]
    all_gather x1, waiting for transfers between devices: 36.6 us -> 18 us  [local(): gathered = lax.all_gather(keyvals, 'wide', axis=0, tiled=True)]
    unnamed x15 -> x13, waiting for transfers between devices: 82.5 us -> 97.6 us
    gather x0 -> x2, local copies, waits for them, and re-layouts: none -> 8.2 us  [ring_gather(): blocks = jnp.stack(blocks)[(index - jnp.arange(size)) % size]]
  transfers between devices with their start and end apart: 13 -> 25, of which waited for: 13 -> 22; matrix products, arithmetic and copies ran while one was open for 8% -> 10% of each run, Pallas kernels for 0% -> 0%
where the time goes in v1:
time: 490 us; the launch traced here: 489 us
  waiting for transfers between devices  380 us (78%)
  matrix products  42.2 us (9%)
  local copies, waits for them, and re-layouts  31.9 us (7%)
  between operations  17 us (3%)
  other arithmetic  16.9 us (3%)
    ppermute x14, waiting for transfers between devices, ring_gather(): blocks.append(lax.ppermute(blocks[-1], axis, right))  157 us
    unnamed x13, waiting for transfers between devices  97.6 us
    all_gather x3, waiting for transfers between devices, fold_rows(): lax.all_gather(second_weight, 'wide', axis=0, tiled=True)  53.8 us
    all_gather x2, waiting for transfers between devices, add_branch(): result_rows = lax.all_gather(updated, 'narrow', axis=1, tiled=True)  30.9 us
    all_gather x3, waiting for transfers between devices, fold_rows(): lax.all_gather(first_weight, 'wide', axis=0, tiled=True)  22.4 us
    all_gather x1, waiting for transfers between devices, local(): gathered = lax.all_gather(keyvals, 'wide', axis=0, tiled=True)  18 us
    dot_general x2, matrix products, column_terms(): jnp.dot(left_rows, ring_gather(weight_block, 'wide', 1), preferred_elemen...  16.9 us
    dot_general x3, matrix products, fold_rows(): jnp.dot(normed, lax.all_gather(first_weight, 'wide', axis=0, tiled=True),...  15.3 us
  transfers between devices with their start and end apart: 25, of which 22 were waited for; matrix products, arithmetic and copies ran while one was open for 10% of the time, Pallas kernels for 0%

profile of v1, /device:TPU:0, one launch (start us, length us, event | category | flops | bytes accessed | tf_op | source)
XLA Modules:
  0.0 489.4 jit_solution(898228354492659247)
XLA Ops:
  13.2 25.1 %all-gather.10.cloned.1.call-done = bf16[1536,512]{1,0:T(8,128)(2,1)} async-done(((bf16[192,512]{1,0:T(8,128)(2,1)}), bf16[1536,512]{1,0:T(8,128)(2,1)}) %all-gather.10.cloned.1.call-update) | async-done | bytes 1572880 | tf_op jit(solution)/shard_map/all_gather | solution.py:68
  49.0 5.3 %collective-permute-done.1 = bf16[384,192]{0,1:T(8,128)(2,1)S(1)} collective-permute-done((bf16[384,192]{0,1:T(8,128)(2,1)S(1)}, bf16[384,192]{0,1:T(8,128)(2,1)S(1)}, u32[]{:S(2)}, u32[]{:S(2)}) %collective-permute-start.1) | collective-permute-done | bytes 147488 | tf_op jit(solution)/shard_map/ppermute | solution.py:25
  54.3 5.4 %collective-permute-done.2 = bf16[384,192]{0,1:T(8,128)(2,1)S(1)} collective-permute-done((bf16[384,192]{0,1:T(8,128)(2,1)S(1)}, bf16[384,192]{0,1:T(8,128)(2,1)S(1)}, u32[]{:S(2)}, u32[]{:S(2)}) %collective-permute-start.2) | collective-permute-done | bytes 147488 | tf_op jit(solution)/shard_map/ppermute | solution.py:25
  59.8 6.1 %collective-permute-done.3 = bf16[384,192]{0,1:T(8,128)(2,1)S(1)} collective-permute-done((bf16[384,192]{0,1:T(8,128)(2,1)S(1)}, bf16[384,192]{0,1:T(8,128)(2,1)S(1)}, u32[]{:S(2)}, u32[]{:S(2)}) %collective-permute-start.3) | collective-permute-done | bytes 147488 | tf_op jit(solution)/shard_map/ppermute | solution.py:25
  66.0 5.4 %collective-permute-done.4 = bf16[384,192]{0,1:T(8,128)(2,1)S(1)} collective-permute-done((bf16[384,192]{0,1:T(8,128)(2,1)S(1)}, bf16[384,192]{0,1:T(8,128)(2,1)S(1)}, u32[]{:S(2)}, u32[]{:S(2)}) %collective-permute-start.4) | collective-permute-done | bytes 147488 | tf_op jit(solution)/shard_map/ppermute | solution.py:25
  71.4 5.4 %collective-permute-done.5 = bf16[384,192]{0,1:T(8,128)(2,1)S(1)} collective-permute-done((bf16[384,192]{0,1:T(8,128)(2,1)S(1)}, bf16[384,192]{0,1:T(8,128)(2,1)S(1)}, u32[]{:S(2)}, u32[]{:S(2)}) %collective-permute-start.5) | collective-permute-done | bytes 147488 | tf_op jit(solution)/shard_map/ppermute | solution.py:25
  76.9 8.2 %collective-permute-done.6 = bf16[384,192]{0,1:T(8,128)(2,1)S(1)} collective-permute-done((bf16[384,192]{0,1:T(8,128)(2,1)S(1)}, bf16[384,192]{0,1:T(8,128)(2,1)S(1)}, u32[]{:S(2)}, u32[]{:S(2)}) %collective-permute-start.6) | collective-permute-done | bytes 147488 | tf_op jit(solution)/shard_map/ppermute | solution.py:25
  89.0 18.0 %all-gather.12.cloned.1.call-done = bf16[4096,512]{1,0:T(8,128)(2,1)} async-done(((bf16[512,512]{1,0:T(8,128)(2,1)}), bf16[4096,512]{1,0:T(8,128)(2,1)}) %all-gather.12.cloned.1.call-update) | async-done | bytes 4194320 | tf_op jit(solution)/shard_map/all_gather | solution.py:217
  110.6 5.7 %while.15 = (s32[]{:T(128)}, f32[1536]{0:T(1024)S(1)}, f32[1536]{0:T(1024)S(1)}, f32[1536,128]{1,0:T(8,128)S(1)}, s32[]{:T(128)}, /*index=5*/s32[8]{0:T(128)S(1)...) while((s32[]{:T(128)}, f32[1536]{0:T(1024)S(1)}, ...), condition=%wide.region_7.8_spmd.clone, body=%wide.region_3.7_spmd.clone.sunk | while | flops 419576320 | bytes 11870495 | solution.py:147
  119.5 58.3 %reduce-scatter.7.cloned.1.call-done = bf16[384,512]{1,0:T(8,128)(2,1)} async-done(((bf16[1536,512]{1,0:T(8,128)(2,1)}), bf16[384,512]{1,0:T(8,128)(2,1)}) %reduce-scatter.7.cloned.1.call-update) | async-done | bytes 393232
  182.3 13.4 %collective-permute-done.7 = bf16[2240,192]{0,1:T(8,128)(2,1)S(1)} collective-permute-done((bf16[2240,192]{0,1:T(8,128)(2,1)S(1)}, bf16[2240,192]{0,1:T(8,128)(2,1)S(1)}, u32[]{:S(2)}, u32[]{:S(2)}) %collective-permute-start.7) | collective-permute-done | bytes 860192 | tf_op jit(solution)/shard_map/ppermute | solution.py:25
  195.6 13.4 %collective-permute-done.8 = bf16[2240,192]{0,1:T(8,128)(2,1)S(1)} collective-permute-done((bf16[2240,192]{0,1:T(8,128)(2,1)S(1)}, bf16[2240,192]{0,1:T(8,128)(2,1)S(1)}, u32[]{:S(2)}, u32[]{:S(2)}) %collective-permute-start.8) | collective-permute-done | bytes 860192 | tf_op jit(solution)/shard_map/ppermute | solution.py:25
  209.0 13.4 %collective-permute-done.9 = bf16[2240,192]{0,1:T(8,128)(2,1)S(1)} collective-permute-done((bf16[2240,192]{0,1:T(8,128)(2,1)S(1)}, bf16[2240,192]{0,1:T(8,128)(2,1)S(1)}, u32[]{:S(2)}, u32[]{:S(2)}) %collective-permute-start.9) | collective-permute-done | bytes 860192 | tf_op jit(solution)/shard_map/ppermute | solution.py:25
  223.4 21.8 %collective-permute-done.10 = bf16[2240,192]{0,1:T(8,128)(2,1)S(1)} collective-permute-done((bf16[2240,192]{0,1:T(8,128)(2,1)S(1)}, bf16[2240,192]{0,1:T(8,128)(2,1)S(1)}, u32[]{:S(2)}, u32[]{:S(2)}) %collective-permute-start.10) | collective-permute-done | bytes 860192 | tf_op jit(solution)/shard_map/ppermute | solution.py:25
  247.2 26.5 %collective-permute-done.11 = bf16[2240,192]{0,1:T(8,128)(2,1)S(1)} collective-permute-done((bf16[2240,192]{0,1:T(8,128)(2,1)S(1)}, bf16[2240,192]{0,1:T(8,128)(2,1)S(1)}, u32[]{:S(2)}, u32[]{:S(2)}) %collective-permute-start.11) | collective-permute-done | bytes 860192 | tf_op jit(solution)/shard_map/ppermute | solution.py:25
  275.7 11.3 %collective-permute-done.12 = bf16[2240,192]{0,1:T(8,128)(2,1)S(1)} collective-permute-done((bf16[2240,192]{0,1:T(8,128)(2,1)S(1)}, bf16[2240,192]{0,1:T(8,128)(2,1)S(1)}, u32[]{:S(2)}, u32[]{:S(2)}) %collective-permute-start.12) | collective-permute-done | bytes 860192 | tf_op jit(solution)/shard_map/ppermute | solution.py:25
  289.0 20.9 %collective-permute-done.13 = bf16[2240,192]{0,1:T(8,128)(2,1)S(1)} collective-permute-done((bf16[2240,192]{0,1:T(8,128)(2,1)S(1)}, bf16[2240,192]{0,1:T(8,128)(2,1)S(1)}, u32[]{:S(2)}, u32[]{:S(2)}) %collective-permute-start.13) | collective-permute-done | bytes 860192 | tf_op jit(solution)/shard_map/ppermute | solution.py:25
  310.9 7.4 %gather_fusion.1 = bf16[8,2240,192]{1,2,0:T(8,128)(2,1)} fusion(bf16[8,2240,192]{1,2,0:T(8,128)(2,1)} %bitcast_dynamic-update-slice_fusion, s32[1024]{0:T(1024)S(1)} %pad_clamp_fusion.1), kind=kCustom, calls=%fused_computation.1 | custom fusion | bytes 13762592 | tf_op jit(solution)/shard_map/gather | solution.py:27
  320.2 9.6 %fusion.28 = f32[512,2240]{0,1:T(8,128)} fusion(bf16[1536,2240]{1,0:T(8,128)(2,1)} %all-gather.18.cloned.1.call-done, bf16[512,1536]{1,0:T(8,128)(2,1)} %all-gather.16.cloned.1.call-done, f32[1536]{0:T(1024)S(1)} %convert_element_type.121, f32[512]{0:T(512)S(1)} %add_rsqrt_fusion.1), kind=kOutput, calls=%fused_computation.62 | convolution fusion | flops 3526361088 | bytes 13049856 | tf_op jit(solution)/shard_map/dot_general | solution.py:61
  333.9 15.9 %convolution_convert_fusion = bf16[512,1536]{1,0:T(8,128)(2,1)} fusion(bf16[2240,1536]{0,1:T(8,128)(2,1)} %bitcast.89, bf16[1536,2240]{1,0:T(8,128)(2,1)} %all-gather.20.cloned.1.call-done, f32[512,2240]{0,1:T(8,128)} %fusion.28, bf16[512,1536]{1,0:T(8,128)(2,1)S(1)} %copy-done.2, f32[1536]{0:T(1024)S(1)} %convert_element_type.121, f32[512]{0:T(512)S(1)} %add_rsqrt_fusion.1), kind=kOutput, calls=%fused_computation.42 | convolution fusion | flops 7057244160 | bytes 21504000 | tf_op jit(solution)/shard_map/dot_general | solution.py:75
  352.6 35.4 %reduce-scatter.9.cloned.1.call-done = bf16[384,512]{1,0:T(8,128)(2,1)} async-done(((bf16[1536,512]{1,0:T(8,128)(2,1)}), bf16[384,512]{1,0:T(8,128)(2,1)}) %reduce-scatter.9.cloned.1.call-update) | async-done | bytes 393232
  395.5 30.9 %all-gather.22.cloned.1.call-done = bf16[512,1536]{1,0:T(8,128)(2,1)} async-done(((bf16[512,384]{1,0:T(8,128)(2,1)}), bf16[512,1536]{1,0:T(8,128)(2,1)}) %all-gather.22.cloned.1.call-update) | async-done | bytes 1572880 | tf_op jit(solution)/shard_map/all_gather | solution.py:93
  428.1 24.6 %all-gather.26.cloned.1.call-done = bf16[1536,512]{1,0:T(8,128)(2,1)} async-done(((bf16[192,512]{1,0:T(8,128)(2,1)}), bf16[1536,512]{1,0:T(8,128)(2,1)}) %all-gather.26.cloned.1.call-update) | async-done | bytes 1572880 | tf_op jit(solution)/shard_map/all_gather | solution.py:68
  456.3 22.4 %all-gather.24.cloned.1.call-done = bf16[1536,384]{1,0:T(8,128)(2,1)} async-done(((bf16[192,384]{1,0:T(8,128)(2,1)}), bf16[1536,384]{1,0:T(8,128)(2,1)}) %all-gather.24.cloned.1.call-update) | async-done | bytes 1179664 | tf_op jit(solution)/shard_map/all_gather | solution.py:63
  (161 shorter events, 68.3 us)
Async XLA Ops:
  7.2 31.1 %all-gather.10.cloned.1.call-start = ((), (), s32[]{:S(2)}) async-start(), calls=%async_computation.2 | async-start | bytes 1769472 | tf_op jit(solution)/shard_map/all_gather | solution.py:68
  7.9 78.1 %all-gather.14.cloned.1.call-start = ((), (), s32[]{:S(2)}) async-start(), calls=%async_computation.4 | async-start | bytes 1327104 | tf_op jit(solution)/shard_map/all_gather | solution.py:63
  8.6 98.4 %all-gather.12.cloned.1.call-start = ((), (), s32[]{:S(2)}) async-start(), calls=%async_computation.3 | async-start | bytes 4718592 | tf_op jit(solution)/shard_map/all_gather | solution.py:217
  42.7 135.1 %reduce-scatter.7.cloned.1.call-start = ((), (), s32[]{:S(2)}) async-start(), calls=%async_computation.11 | async-start | bytes 1966080
  42.7 5.5 %collective-permute-start = (bf16[384,192]{0,1:T(8,128)(2,1)S(1)}, bf16[384,192]{0,1:T(8,128)(2,1)S(1)}, u32[]{:S(2)}, u32[]{:S(2)}) collective-permute-start(bf16[384,192]{0,1:T(8,128)(2,1)S(1)} %copy-done.4), channel_id=1, source_target_pairs={{0,4},{4,8},{8,12},{12,16},{16,20},{20,24},{24,28},{28,0},{1,5},{5... | collective-permute-start | bytes 442376 | tf_op jit(solution)/shard_map/ppermute | solution.py:25
  48.2 6.1 %collective-permute-start.1 = (bf16[384,192]{0,1:T(8,128)(2,1)S(1)}, bf16[384,192]{0,1:T(8,128)(2,1)S(1)}, u32[]{:S(2)}, u32[]{:S(2)}) collective-permute-start(bf16[384,192]{0,1:T(8,128)(2,1)S(1)} %collective-permute-done), channel_id=1, source_target_pairs={{0,4},{4,8},{8,12},{12,16},{16,20},{20,24},{24,28},{28,0},{1,5},{5... | collective-permute-start | bytes 442376 | tf_op jit(solution)/shard_map/ppermute | solution.py:25
  54.3 5.5 %collective-permute-start.2 = (bf16[384,192]{0,1:T(8,128)(2,1)S(1)}, bf16[384,192]{0,1:T(8,128)(2,1)S(1)}, u32[]{:S(2)}, u32[]{:S(2)}) collective-permute-start(bf16[384,192]{0,1:T(8,128)(2,1)S(1)} %collective-permute-done.1), channel_id=1, source_target_pairs={{0,4},{4,8},{8,12},{12,16},{16,20},{20,24},{24,28},{28,0},{1,5},{5... | collective-permute-start | bytes 442376 | tf_op jit(solution)/shard_map/ppermute | solution.py:25
  59.8 6.2 %collective-permute-start.3 = (bf16[384,192]{0,1:T(8,128)(2,1)S(1)}, bf16[384,192]{0,1:T(8,128)(2,1)S(1)}, u32[]{:S(2)}, u32[]{:S(2)}) collective-permute-start(bf16[384,192]{0,1:T(8,128)(2,1)S(1)} %collective-permute-done.2), channel_id=1, source_target_pairs={{0,4},{4,8},{8,12},{12,16},{16,20},{20,24},{24,28},{28,0},{1,5},{5... | collective-permute-start | bytes 442376 | tf_op jit(solution)/shard_map/ppermute | solution.py:25
  71.4 5.5 %collective-permute-start.5 = (bf16[384,192]{0,1:T(8,128)(2,1)S(1)}, bf16[384,192]{0,1:T(8,128)(2,1)S(1)}, u32[]{:S(2)}, u32[]{:S(2)}) collective-permute-start(bf16[384,192]{0,1:T(8,128)(2,1)S(1)} %collective-permute-done.4), channel_id=1, source_target_pairs={{0,4},{4,8},{8,12},{12,16},{16,20},{20,24},{24,28},{28,0},{1,5},{5... | collective-permute-start | bytes 442376 | tf_op jit(solution)/shard_map/ppermute | solution.py:25
  76.9 8.2 %collective-permute-start.6 = (bf16[384,192]{0,1:T(8,128)(2,1)S(1)}, bf16[384,192]{0,1:T(8,128)(2,1)S(1)}, u32[]{:S(2)}, u32[]{:S(2)}) collective-permute-start(bf16[384,192]{0,1:T(8,128)(2,1)S(1)} %collective-permute-done.5), channel_id=1, source_target_pairs={{0,4},{4,8},{8,12},{12,16},{16,20},{20,24},{24,28},{28,0},{1,5},{5... | collective-permute-start | bytes 442376 | tf_op jit(solution)/shard_map/ppermute | solution.py:25
  119.4 198.8 %all-gather.16.cloned.1.call-start = ((), (), s32[]{:S(2)}) async-start(), calls=%async_computation.5 | async-start | bytes 1966080 | tf_op jit(solution)/shard_map/all_gather | solution.py:93
  180.8 139.4 %all-gather.18.cloned.1.call-start = ((), (), s32[]{:S(2)}) async-start(), calls=%async_computation.6 | async-start | bytes 7962624 | tf_op jit(solution)/shard_map/all_gather | solution.py:63
  181.4 152.5 %all-gather.20.cloned.1.call-start = ((), (), s32[]{:S(2)}) async-start(), calls=%async_computation.7 | async-start | bytes 7962624 | tf_op jit(solution)/shard_map/all_gather | solution.py:68
  182.2 205.9 %reduce-scatter.9.cloned.1.call-start = ((), (), s32[]{:S(2)}) async-start(), calls=%async_computation.12 | async-start | bytes 1966080
  182.2 13.4 %collective-permute-start.7 = (bf16[2240,192]{0,1:T(8,128)(2,1)S(1)}, bf16[2240,192]{0,1:T(8,128)(2,1)S(1)}, u32[]{:S(2)}, u32[]{:S(2)}) collective-permute-start(bf16[2240,192]{0,1:T(8,128)(2,1)S(1)} %copy-done.3), channel_id=1, source_target_pairs={{0,4},{4,8},{8,12},{12,16},{16,20},{20,24},{24,28},{28,0},{1,5},{5... | collective-permute-start | bytes 2580488 | tf_op jit(solution)/shard_map/ppermute | solution.py:25
  195.6 13.4 %collective-permute-start.8 = (bf16[2240,192]{0,1:T(8,128)(2,1)S(1)}, bf16[2240,192]{0,1:T(8,128)(2,1)S(1)}, u32[]{:S(2)}, u32[]{:S(2)}) collective-permute-start(bf16[2240,192]{0,1:T(8,128)(2,1)S(1)} %collective-permute-done.7), channel_id=1, source_target_pairs={{0,4},{4,8},{8,12},{12,16},{16,20},{20,24},{24,28},{28,0},{1,5},{5... | collective-permute-start | bytes 2580488 | tf_op jit(solution)/shard_map/ppermute | solution.py:25
  209.0 13.4 %collective-permute-start.9 = (bf16[2240,192]{0,1:T(8,128)(2,1)S(1)}, bf16[2240,192]{0,1:T(8,128)(2,1)S(1)}, u32[]{:S(2)}, u32[]{:S(2)}) collective-permute-start(bf16[2240,192]{0,1:T(8,128)(2,1)S(1)} %collective-permute-done.8), channel_id=1, source_target_pairs={{0,4},{4,8},{8,12},{12,16},{16,20},{20,24},{24,28},{28,0},{1,5},{5... | collective-permute-start | bytes 2580488 | tf_op jit(solution)/shard_map/ppermute | solution.py:25
  222.4 22.8 %collective-permute-start.10 = (bf16[2240,192]{0,1:T(8,128)(2,1)S(1)}, bf16[2240,192]{0,1:T(8,128)(2,1)S(1)}, u32[]{:S(2)}, u32[]{:S(2)}) collective-permute-start(bf16[2240,192]{0,1:T(8,128)(2,1)S(1)} %collective-permute-done.9), channel_id=1, source_target_pairs={{0,4},{4,8},{8,12},{12,16},{16,20},{20,24},{24,28},{28,0},{1,5},{5... | collective-permute-start | bytes 2580488 | tf_op jit(solution)/shard_map/ppermute | solution.py:25
  245.2 28.4 %collective-permute-start.11 = (bf16[2240,192]{0,1:T(8,128)(2,1)S(1)}, bf16[2240,192]{0,1:T(8,128)(2,1)S(1)}, u32[]{:S(2)}, u32[]{:S(2)}) collective-permute-start(bf16[2240,192]{0,1:T(8,128)(2,1)S(1)} %collective-permute-done.10), channel_id=1, source_target_pairs={{0,4},{4,8},{8,12},{12,16},{16,20},{20,24},{24,28},{28,0},{1,5},{5... | collective-permute-start | bytes 2580488 | tf_op jit(solution)/shard_map/ppermute | solution.py:25
  273.7 13.4 %collective-permute-start.12 = (bf16[2240,192]{0,1:T(8,128)(2,1)S(1)}, bf16[2240,192]{0,1:T(8,128)(2,1)S(1)}, u32[]{:S(2)}, u32[]{:S(2)}) collective-permute-start(bf16[2240,192]{0,1:T(8,128)(2,1)S(1)} %collective-permute-done.11), channel_id=1, source_target_pairs={{0,4},{4,8},{8,12},{12,16},{16,20},{20,24},{24,28},{28,0},{1,5},{5... | collective-permute-start | bytes 2580488 | tf_op jit(solution)/shard_map/ppermute | solution.py:25
  287.0 22.8 %collective-permute-start.13 = (bf16[2240,192]{0,1:T(8,128)(2,1)S(1)}, bf16[2240,192]{0,1:T(8,128)(2,1)S(1)}, u32[]{:S(2)}, u32[]{:S(2)}) collective-permute-start(bf16[2240,192]{0,1:T(8,128)(2,1)S(1)} %collective-permute-done.12), channel_id=1, source_target_pairs={{0,4},{4,8},{8,12},{12,16},{16,20},{20,24},{24,28},{28,0},{1,5},{5... | collective-permute-start | bytes 2580488 | tf_op jit(solution)/shard_map/ppermute | solution.py:25
  352.6 73.8 %all-gather.22.cloned.1.call-start = ((), (), s32[]{:S(2)}) async-start(), calls=%async_computation.8 | async-start | bytes 1966080 | tf_op jit(solution)/shard_map/all_gather | solution.py:93
  390.1 62.6 %all-gather.26.cloned.1.call-start = ((), (), s32[]{:S(2)}) async-start(), calls=%async_computation.10 | async-start | bytes 1769472 | tf_op jit(solution)/shard_map/all_gather | solution.py:68
  390.7 88.0 %all-gather.24.cloned.1.call-start = ((), (), s32[]{:S(2)}) async-start(), calls=%async_computation.9 | async-start | bytes 1327104 | tf_op jit(solution)/shard_map/all_gather | solution.py:63
  (15 other events, 500.2 us)
Sparse Core Ops, SparseCore 0:
  9.9 28.3 all-gather.9
  40.2 25.0 all-gather.13
  67.8 39.2 all-gather.11
  119.5 58.1 reduce-scatter.6
  180.9 36.0 all-gather.15
  218.8 60.6 all-gather.17
  281.4 52.4 all-gather.19
  352.7 35.2 reduce-scatter.8
  390.2 36.0 all-gather.21
  428.1 24.6 all-gather.25
  454.6 24.0 all-gather.23
